TPU v7x, 32 devices: a whole 2x2x4 slice. The times are simulated.
32 devices in a mesh: row: 8 (over z, y), col: 4 (over x, core).
Axes of the slice: x: 2, y: 2, z: 4, core: 2. Of those that a mesh axis runs over, the one named last changes fastest.
Arguments:
- query_acts: bfloat16 [256, 8192], P('col', 'row'), may hold values from -6 to 6
- query_grads: bfloat16 [256, 28672], P('row', 'col'), may hold values from -6 to 6
- ritz_mats: float32 [3, 8192, 28672], P(None, 'row', 'col'), may hold values from -0.095683193 to 0.095683193, as said below
- eigenvalues: float32 [3], replicated, may hold values from 0.5 to 4
- train_acts: bfloat16 [64, 8192], P('row'), may hold values from -6 to 6
- train_grads: bfloat16 [64, 28672], P('row', 'col'), may hold values from -6 to 6
Outputs:
- response: bfloat16 [64, 28672], P('row', 'col')
- scores: float32 [64], P('row')
Inputs may be any that keep to these rules, and one draw needn't show every extreme that they name: `ritz_mats`: real entries of order one over the square root of 8192; every matrix has full rank.
All inputs are finite; a program needn't handle non-finite values.
Results may differ from a plain program's by a relative error of at most 0.0012.
Values may be sent and summed in bfloat16 or wider, within the bound.
No kernel may reach another device: no remote copies, remote signals or barrier semaphores. Data moves between devices by JAX's collectives and lax.ppermute only.
A program may use at most 192 MiB of HBM per device.

v0:
```python
import math
import jax
import jax.numpy as jnp
from jax import lax
from jax.sharding import PartitionSpec as P

D_OUT = 28672
QUERY = 256
highest = lax.Precision.HIGHEST


def per_device(query_acts, query_grads, ritz_mats, eigenvalues, train_acts, train_grads):
    outer_cols = ritz_mats.shape[2]
    acts_all = lax.all_gather(query_acts, "col", axis=0, tiled=True)
    grad_tile = lax.dot_general(
        acts_all,
        lax.all_gather(query_grads, "row", axis=0, tiled=True),
        (((0,), (0,)), ((), ())),
        preferred_element_type=jnp.float32,
    )
    local_terms = jnp.sum(ritz_mats * grad_tile[None], axis=(1, 2))
    coeffs = lax.psum(local_terms, ("row", "col"))
    weights = coeffs / (eigenvalues * math.sqrt(QUERY * D_OUT))
    train_local = lax.all_to_all(train_acts, "row", split_axis=1, concat_axis=0, tiled=True).astype(
        jnp.float32
    )
    root_width = math.sqrt(D_OUT)
    total = jnp.zeros((lax.axis_size("row") * train_acts.shape[0], outer_cols), jnp.float32)
    for which in range(ritz_mats.shape[0]):
        total = total + weights[which] * jnp.dot(train_local, ritz_mats[which], precision=highest)
    response_full = lax.psum_scatter(total, "row", scatter_dimension=0, tiled=True)
    score_terms = jnp.sum(response_full * train_grads.astype(jnp.float32), axis=1) / root_width
    scores = lax.psum(score_terms, "col")
    response = response_full.astype(jnp.bfloat16)
    return (response, scores)


def solution(mesh):
    in_specs = (
        P("col", "row"),
        P("row", "col"),
        P(None, "row", "col"),
        P(),
        P("row", None),
        P("row", "col"),
    )
    out_specs = (P("row", "col"), P("row"))
    return jax.shard_map(
        per_device, mesh=mesh, in_specs=in_specs, out_specs=out_specs, check_vma=False
    )
```

profile of v0, /device:TPU:0, one launch (start us, length us, event | category | flops | bytes accessed | tf_op | source)
XLA Modules:
  0.0 306.3 jit_solution(11983988093099938950)
XLA Ops:
  7.2 0.0 all-gather.2.cloned.1.call-start
  7.2 0.7 all-gather.2.cloned.1.call-update
  7.9 8.9 %all_gather.6 = bf16[256,1024]{1,0:T(8,128)(2,1)S(1)} all-gather(bf16[64,1024]{1,0:T(8,128)(2,1)} %param.6), channel_id=1, replica_groups=mesh['row'=8,'col'=4] {'col'}, dimensions={0}, use_global_device_ids=true | all-gather | bytes 655360 | tf_op jit(solution)/shard_map/all_gather | solution.py:14
  16.8 62.4 %all-gather.2.cloned.1.call-done = bf16[256,7168]{1,0:T(8,128)(2,1)} async-done(((bf16[32,7168]{1,0:T(8,128)(2,1)}), bf16[256,7168]{1,0:T(8,128)(2,1)}) %all-gather.2.cloned.1.call-update) | async-done | bytes 3670032 | tf_op jit(solution)/shard_map/all_gather | solution.py:17
  79.1 13.7 %fusion.28 = f32[1024,7168]{1,0:T(8,128)} fusion(bf16[256,1024]{1,0:T(8,128)(2,1)S(1)} %all_gather.6, bf16[256,7168]{1,0:T(8,128)(2,1)} %all-gather.2.cloned.1.call-done), kind=kOutput, calls=%fused_computation.22 | convolution fusion | flops 3758096384 | bytes 33554432 | tf_op jit(solution)/shard_map/dot_general | solution.py:15
  92.8 0.0 copy-start.1
  92.8 35.5 %multiply_reduce_fusion = f32[3]{0:T(128)S(1)} fusion(f32[3,1024,7168]{2,1,0:T(8,128)} %param.8, f32[1024,7168]{1,0:T(8,128)} %fusion.28), kind=kLoop, calls=%fused_computation | loop fusion | flops 44040188 | bytes 117440528 | tf_op jit(solution)/shard_map/reduce_sum | solution.py:21
  128.4 3.4 %all-to-all-start = ((bf16[8,8,1024]{2,0,1:T(8,128)(2,1)}), bf16[8,8,1024]{2,0,1:T(8,128)(2,1)S(1)}, u32[]{:S(2)}, u32[]{:S(2)}) async-start(bf16[8,8,1024]{2,0,1:T(8,128)(2,1)} %bitcast.1), calls=%async_computation | async-start | bytes 262144 | tf_op jit(solution)/shard_map/all_to_all | solution.py:24
  131.8 0.0 reduce-scatter.2.cloned.1.call-start
  131.8 40.7 %psum.14 = f32[3]{0:T(128)S(1)} all-reduce(f32[3]{0:T(128)S(1)} %multiply_reduce_fusion), channel_id=1, replica_groups=mesh['row'=8,'col'=4] {'row','col'}, use_global_device_ids=true, to_apply=%region_1.0 | all-reduce | flops 3 | bytes 24 | tf_op jit(solution)/shard_map/psum | solution.py:22
  172.5 0.0 copy-done.1
  172.5 0.7 fusion.27
  173.2 0.0 all-to-all-done
  173.2 15.6 %fusion.15 = f32[64,7168]{1,0:T(8,128)S(1)} fusion(f32[3,1024,7168]{2,1,0:T(8,128)} %param.8, f32[]{:T(128)} %bitcast.5, bf16[8,8,1024]{2,0,1:T(8,128)(2,1)S(1)} %all-to-all-done), kind=kOutput, calls=%fused_computation.12 | convolution fusion | flops 5637603328 | bytes 31326720 | tf_op jit(solution)/shard_map/dot_general | solution.py:30
  188.8 18.0 %fusion.12 = f32[64,7168]{1,0:T(8,128)S(1)} fusion(f32[64,7168]{1,0:T(8,128)S(1)} %fusion.15, f32[3,1024,7168]{2,1,0:T(8,128)} %param.8, f32[]{:T(128)} %bitcast, bf16[8,8,1024]{2,0,1:T(8,128)(2,1)S(1)} %all-to-all-done), kind=kOutput, calls=%fused_computation.11 | convolution fusion | flops 5638062080 | bytes 33161728 | tf_op jit(solution)/shard_map/dot_general | solution.py:30
  206.8 0.0 copy-start
  206.8 17.5 %fusion.21 = f32[64,7168]{1,0:T(8,128)} fusion(f32[64,7168]{1,0:T(8,128)S(1)} %fusion.12, f32[3,1024,7168]{2,1,0:T(8,128)} %param.8, f32[]{:T(128)} %bitcast.8, bf16[8,8,1024]{2,0,1:T(8,128)(2,1)S(1)} %all-to-all-done), kind=kOutput, calls=%fused_computation.14 | convolution fusion | flops 5638062080 | bytes 33161728 | tf_op jit(solution)/shard_map/dot_general | solution.py:30
  224.3 0.0 reduce-scatter.2.cloned.1.call-update
  224.3 67.2 %reduce-scatter.2.cloned.1.call-done = f32[8,7168]{1,0:T(8,128)} async-done(((f32[64,7168]{1,0:T(8,128)}), f32[8,7168]{1,0:T(8,128)}) %reduce-scatter.2.cloned.1.call-update) | async-done | bytes 229392 | tf_op jit(solution)/shard_map/reduce_scatter | solution.py:31
  291.5 0.0 copy-done
  291.5 1.8 multiply_reduce_fusion.1
  293.3 6.2 %psum.15 = f32[8]{0:T(128)} all-reduce(f32[8]{0:T(128)S(1)} %broadcast_multiply_fusion), channel_id=1, replica_groups=mesh['row'=8,'col'=4] {'col'}, use_global_device_ids=true, to_apply=%region_4.0 | all-reduce | flops 8 | bytes 64 | tf_op jit(solution)/shard_map/psum | solution.py:33
  (2 shorter events, 0.0 us)
Async XLA Ops:
  7.2 72.0 %all-gather.2.cloned.1.call-start = ((), (), s32[]{:S(2)}) async-start(), calls=%async_computation.2 | async-start | bytes 4128768 | tf_op jit(solution)/shard_map/all_gather | solution.py:17
  92.8 79.7 %copy-start.1 = (f32[3]{0:T(128)S(1)}, f32[3]{0:T(128)}, u32[]{:S(2)}) copy-start(f32[3]{0:T(128)} %param.9) | copy-start | bytes 40
  128.4 44.8 %all-to-all-start = ((bf16[8,8,1024]{2,0,1:T(8,128)(2,1)}), bf16[8,8,1024]{2,0,1:T(8,128)(2,1)S(1)}, u32[]{:S(2)}, u32[]{:S(2)}) async-start(bf16[8,8,1024]{2,0,1:T(8,128)(2,1)} %bitcast.1), calls=%async_computation | async-start | bytes 262144 | tf_op jit(solution)/shard_map/all_to_all | solution.py:24
  131.8 159.8 %reduce-scatter.2.cloned.1.call-start = ((), (), s32[]{:S(2)}) async-start(), calls=%async_computation.3 | async-start | bytes 2064384 | tf_op jit(solution)/shard_map/reduce_scatter | solution.py:31
  206.8 84.7 %copy-start = (bf16[8,7168]{1,0:T(8,128)(2,1)S(1)}, bf16[8,7168]{1,0:T(8,128)(2,1)}, u32[]{:S(2)}) copy-start(bf16[8,7168]{1,0:T(8,128)(2,1)} %param.11) | copy-start | bytes 344068
Sparse Core Ops, SparseCore 0:
  10.2 68.9 all-gather.1
  224.4 67.0 reduce-scatter.1
where the time goes:
time: 307 us; the launch traced here: 306 us
  waiting for transfers between devices  130 us (42%)
  matrix products  64.8 us (21%)
  blocking collectives  55.7 us (18%)
  other arithmetic  37.4 us (12%)
  between operations  14.1 us (5%)
  starting transfers between devices  3.46 us (1%)
    reduce_scatter x1, waiting for transfers between devices, per_device(): lax.psum_scatter(total, 'row', scatter_dimension=0, tiled=True)  67.2 us
    all_gather x1, waiting for transfers between devices, per_device(): lax.all_gather(query_grads, 'row', axis=0, tiled=True)  62.4 us
    dot_general x3, matrix products, per_device(): jnp.dot(train_local, ritz_mats[which], precision=highest)  51.1 us
    psum x1, blocking collectives, per_device(): coeffs = lax.psum(local_terms, ('row', 'col'))  40.7 us
    reduce_sum x1, other arithmetic, per_device(): local_terms = jnp.sum(ritz_mats * grad_tile[None], axis=(1, 2))  35.5 us
    dot_general x1, matrix products, per_device(): lax.dot_general(acts_all, lax.all_gather(query_grads, 'row', axis=0, tile...  13.7 us
    all_gather x1, blocking collectives, per_device(): acts_all = lax.all_gather(query_acts, 'col', axis=0, tiled=True)  8.86 us
    psum x1, blocking collectives, per_device(): scores = lax.psum(score_terms, 'col')  6.17 us
  transfers between devices with their start and end apart: 3, of which 2 were waited for; matrix products, arithmetic and copies ran while one was open for 0% of the time, Pallas kernels for 0%

commit v1 on v0

--- a/solution.py
+++ b/solution.py
@@ -19,7 +19,7 @@
         preferred_element_type=jnp.float32,
     )
     local_terms = jnp.sum(ritz_mats * grad_tile[None], axis=(1, 2))
-    coeffs = lax.psum(local_terms, ("row", "col"))
+    coeffs = jnp.sum(lax.all_gather(local_terms, ("row", "col")), axis=0)
     weights = coeffs / (eigenvalues * math.sqrt(QUERY * D_OUT))
     train_local = lax.all_to_all(train_acts, "row", split_axis=1, concat_axis=0, tiled=True).astype(
         jnp.float32

time: 307 us -> 303 us (0.987)
  waiting for transfers between devices: 130 us -> 125 us
  starting transfers between devices: 3.46 us -> 7.4 us
    psum x1 -> x0, blocking collectives: 40.7 us -> none  [per_device(): coeffs = lax.psum(local_terms, ('row', 'col'))]
    unnamed x0 -> x1, blocking collectives: none -> 39.3 us
    all_gather x1, waiting for transfers between devices: 62.4 us -> 56.5 us  [per_device(): lax.all_gather(query_grads, 'row', axis=0, tiled=True)]
    all_to_all x1, starting transfers between devices: 3.38 us -> 7.32 us  [per_device(): lax.all_to_all(train_acts, 'row', split_axis=1, concat_axis=0, tiled=True)]
  transfers between devices with their start and end apart: 3 -> 3, of which waited for: 2 -> 2; matrix products, arithmetic and copies ran while one was open for 0% -> 17% of each run, Pallas kernels for 0% -> 0%
where the time goes in v1:
time: 303 us; the launch traced here: 302 us
  waiting for transfers between devices  125 us (41%)
  matrix products  64.8 us (21%)
  blocking collectives  52.8 us (17%)
  other arithmetic  37.4 us (12%)
  between operations  14.1 us (5%)
  starting transfers between devices  7.4 us (2%)
    reduce_scatter x1, waiting for transfers between devices, per_device(): lax.psum_scatter(total, 'row', scatter_dimension=0, tiled=True)  67.6 us
    all_gather x1, waiting for transfers between devices, per_device(): lax.all_gather(query_grads, 'row', axis=0, tiled=True)  56.5 us
    dot_general x3, matrix products, per_device(): jnp.dot(train_local, ritz_mats[which], precision=highest)  51.1 us
    unnamed x1, blocking collectives  39.3 us
    reduce_sum x1, other arithmetic, per_device(): local_terms = jnp.sum(ritz_mats * grad_tile[None], axis=(1, 2))  35.5 us
    dot_general x1, matrix products, per_device(): lax.dot_general(acts_all, lax.all_gather(query_grads, 'row', axis=0, tile...  13.7 us
    all_gather x1, blocking collectives, per_device(): acts_all = lax.all_gather(query_acts, 'col', axis=0, tiled=True)  7.38 us
    all_to_all x1, starting transfers between devices, per_device(): lax.all_to_all(train_acts, 'row', split_axis=1, concat_axis=0, tiled=True)  7.32 us
  transfers between devices with their start and end apart: 3, of which 2 were waited for; matrix products, arithmetic and copies ran while one was open for 17% of the time, Pallas kernels for 0%

profile of v1, /device:TPU:0, one launch (start us, length us, event | category | flops | bytes accessed | tf_op | source)
XLA Modules:
  0.0 302.3 jit_solution(11861154336957036385)
XLA Ops:
  7.2 0.0 all-gather.3.cloned.1.call-start
  7.2 0.7 all-gather.3.cloned.1.call-update
  7.9 7.3 %all-to-all-start = ((bf16[8,8,1024]{2,0,1:T(8,128)(2,1)}), bf16[8,8,1024]{2,0,1:T(8,128)(2,1)S(1)}, u32[]{:S(2)}, u32[]{:S(2)}) async-start(bf16[8,8,1024]{2,0,1:T(8,128)(2,1)} %bitcast.34), calls=%async_computation | async-start | bytes 262144 | tf_op jit(solution)/shard_map/all_to_all | solution.py:24
  15.2 0.0 reduce-scatter.2.cloned.1.call-start
  15.3 7.4 %all_gather.12 = bf16[256,1024]{1,0:T(8,128)(2,1)S(1)} all-gather(bf16[64,1024]{1,0:T(8,128)(2,1)} %param.6), channel_id=1, replica_groups=mesh['row'=8,'col'=4] {'col'}, dimensions={0}, use_global_device_ids=true | all-gather | bytes 655360 | tf_op jit(solution)/shard_map/all_gather | solution.py:14
  22.7 56.5 %all-gather.3.cloned.1.call-done = bf16[256,7168]{1,0:T(8,128)(2,1)} async-done(((bf16[32,7168]{1,0:T(8,128)(2,1)}), bf16[256,7168]{1,0:T(8,128)(2,1)}) %all-gather.3.cloned.1.call-update) | async-done | bytes 3670032 | tf_op jit(solution)/shard_map/all_gather | solution.py:17
  79.1 13.7 %fusion.28 = f32[1024,7168]{1,0:T(8,128)} fusion(bf16[256,1024]{1,0:T(8,128)(2,1)S(1)} %all_gather.12, bf16[256,7168]{1,0:T(8,128)(2,1)} %all-gather.3.cloned.1.call-done), kind=kOutput, calls=%fused_computation.22 | convolution fusion | flops 3758096384 | bytes 33554432 | tf_op jit(solution)/shard_map/dot_general | solution.py:15
  92.8 0.0 copy-start.1
  92.8 35.5 %multiply_reduce_fusion = f32[3]{0:T(128)S(1)} fusion(f32[3,1024,7168]{2,1,0:T(8,128)} %param.8, f32[1024,7168]{1,0:T(8,128)} %fusion.28), kind=kLoop, calls=%fused_computation | loop fusion | flops 44040188 | bytes 117440528 | tf_op jit(solution)/shard_map/reduce_sum | solution.py:21
  128.4 0.2 dynamic-update-slice
  128.6 39.3 %all-reduce = f32[96]{0:T(128)S(1)} all-reduce(f32[96]{0:T(128)S(1)} %dynamic-update-slice), channel_id=2, replica_groups=mesh['row'=8,'col'=4] {'row','col'}, use_global_device_ids=true, to_apply=%add | all-reduce | flops 96 | bytes 768
  167.9 0.1 reshape.8
  168.0 0.0 copy-done.1
  168.0 0.7 fusion.27
  168.7 0.0 all-to-all-done
  168.7 15.6 %fusion.15 = f32[64,7168]{1,0:T(8,128)S(1)} fusion(f32[3,1024,7168]{2,1,0:T(8,128)} %param.8, f32[]{:T(128)} %bitcast.5, bf16[8,8,1024]{2,0,1:T(8,128)(2,1)S(1)} %all-to-all-done), kind=kOutput, calls=%fused_computation.12 | convolution fusion | flops 5637603328 | bytes 31326720 | tf_op jit(solution)/shard_map/dot_general | solution.py:30
  184.3 18.0 %fusion.12 = f32[64,7168]{1,0:T(8,128)S(1)} fusion(f32[64,7168]{1,0:T(8,128)S(1)} %fusion.15, f32[3,1024,7168]{2,1,0:T(8,128)} %param.8, f32[]{:T(128)} %bitcast, bf16[8,8,1024]{2,0,1:T(8,128)(2,1)S(1)} %all-to-all-done), kind=kOutput, calls=%fused_computation.11 | convolution fusion | flops 5638062080 | bytes 33161728 | tf_op jit(solution)/shard_map/dot_general | solution.py:30
  202.3 0.0 copy-start
  202.3 17.5 %fusion.21 = f32[64,7168]{1,0:T(8,128)} fusion(f32[64,7168]{1,0:T(8,128)S(1)} %fusion.12, f32[3,1024,7168]{2,1,0:T(8,128)} %param.8, f32[]{:T(128)} %bitcast.8, bf16[8,8,1024]{2,0,1:T(8,128)(2,1)S(1)} %all-to-all-done), kind=kOutput, calls=%fused_computation.14 | convolution fusion | flops 5638062080 | bytes 33161728 | tf_op jit(solution)/shard_map/dot_general | solution.py:30
  219.8 0.0 reduce-scatter.2.cloned.1.call-update
  219.8 67.6 %reduce-scatter.2.cloned.1.call-done = f32[8,7168]{1,0:T(8,128)} async-done(((f32[64,7168]{1,0:T(8,128)}), f32[8,7168]{1,0:T(8,128)}) %reduce-scatter.2.cloned.1.call-update) | async-done | bytes 229392 | tf_op jit(solution)/shard_map/reduce_scatter | solution.py:31
  287.4 0.0 copy-done
  287.5 1.8 multiply_reduce_fusion.1
  289.3 6.2 %psum.7 = f32[8]{0:T(128)} all-reduce(f32[8]{0:T(128)S(1)} %broadcast_multiply_fusion), channel_id=1, replica_groups=mesh['row'=8,'col'=4] {'col'}, use_global_device_ids=true, to_apply=%region_4.0 | all-reduce | flops 8 | bytes 64 | tf_op jit(solution)/shard_map/psum | solution.py:33
  (4 shorter events, 0.0 us)
Async XLA Ops:
  7.2 72.0 %all-gather.3.cloned.1.call-start = ((), (), s32[]{:S(2)}) async-start(), calls=%async_computation.2 | async-start | bytes 4128768 | tf_op jit(solution)/shard_map/all_gather | solution.py:17
  7.9 160.8 %all-to-all-start = ((bf16[8,8,1024]{2,0,1:T(8,128)(2,1)}), bf16[8,8,1024]{2,0,1:T(8,128)(2,1)S(1)}, u32[]{:S(2)}, u32[]{:S(2)}) async-start(bf16[8,8,1024]{2,0,1:T(8,128)(2,1)} %bitcast.34), calls=%async_computation | async-start | bytes 262144 | tf_op jit(solution)/shard_map/all_to_all | solution.py:24
  15.2 272.2 %reduce-scatter.2.cloned.1.call-start = ((), (), s32[]{:S(2)}) async-start(), calls=%async_computation.3 | async-start | bytes 2064384 | tf_op jit(solution)/shard_map/reduce_scatter | solution.py:31
  92.8 75.2 %copy-start.1 = (f32[3]{0:T(128)S(1)}, f32[3]{0:T(128)}, u32[]{:S(2)}) copy-start(f32[3]{0:T(128)} %param.9) | copy-start | bytes 40
  202.3 85.2 %copy-start = (bf16[8,7168]{1,0:T(8,128)(2,1)S(1)}, bf16[8,7168]{1,0:T(8,128)(2,1)}, u32[]{:S(2)}) copy-start(bf16[8,7168]{1,0:T(8,128)(2,1)} %param.11) | copy-start | bytes 344068
Sparse Core Ops, SparseCore 0:
  10.2 68.9 all-gather.2
  219.9 67.4 reduce-scatter.1

commit v2 on v0

--- a/solution.py
+++ b/solution.py
@@ -19,7 +19,7 @@
         preferred_element_type=jnp.float32,
     )
     local_terms = jnp.sum(ritz_mats * grad_tile[None], axis=(1, 2))
-    coeffs = lax.psum(local_terms, ("row", "col"))
+    coeffs = lax.psum(lax.psum(local_terms, "col"), "row")
     weights = coeffs / (eigenvalues * math.sqrt(QUERY * D_OUT))
     train_local = lax.all_to_all(train_acts, "row", split_axis=1, concat_axis=0, tiled=True).astype(
         jnp.float32

time: 307 us -> 291 us (0.948)
  blocking collectives: 55.7 us -> 42.6 us
    psum x1 -> x2, blocking collectives: 40.7 us -> 27.6 us  [per_device(): coeffs = lax.psum(lax.psum(local_terms, 'col'), 'row')]
    reduce_scatter x1, waiting for transfers between devices: 67.2 us -> 64.1 us  [per_device(): lax.psum_scatter(total, 'row', scatter_dimension=0, tiled=True)]
where the time goes in v2:
time: 291 us
  waiting for transfers between devices  127 us (44%)
  matrix products  64.8 us (22%)
  blocking collectives  42.6 us (15%)
  other arithmetic  37.4 us (13%)
  between operations  14.1 us (5%)
  starting transfers between devices  4.1 us (1%)
    reduce_scatter x1, waiting for transfers between devices, per_device(): lax.psum_scatter(total, 'row', scatter_dimension=0, tiled=True)  64.1 us
    all_gather x1, waiting for transfers between devices, per_device(): lax.all_gather(query_grads, 'row', axis=0, tiled=True)  62.4 us
    dot_general x3, matrix products, per_device(): jnp.dot(train_local, ritz_mats[which], precision=highest)  51.1 us
    reduce_sum x1, other arithmetic, per_device(): local_terms = jnp.sum(ritz_mats * grad_tile[None], axis=(1, 2))  35.5 us
    psum x2, blocking collectives, per_device(): coeffs = lax.psum(lax.psum(local_terms, 'col'), 'row')  27.6 us
    dot_general x1, matrix products, per_device(): lax.dot_general(acts_all, lax.all_gather(query_grads, 'row', axis=0, tile...  13.7 us
    all_gather x1, blocking collectives, per_device(): acts_all = lax.all_gather(query_acts, 'col', axis=0, tiled=True)  8.86 us
    psum x1, blocking collectives, per_device(): scores = lax.psum(score_terms, 'col')  6.17 us
  transfers between devices with their start and end apart: 3, of which 2 were waited for; matrix products, arithmetic and copies ran while one was open for 0% of the time, Pallas kernels for 0%

profile of v2, /device:TPU:0, one launch (start us, length us, event | category | flops | bytes accessed | tf_op | source)
XLA Modules:
  0.0 290.8 jit_solution(17317847330949286920)
XLA Ops:
  7.2 0.0 all-gather.2.cloned.1.call-start
  7.2 0.7 all-gather.2.cloned.1.call-update
  7.9 8.9 %all_gather.6 = bf16[256,1024]{1,0:T(8,128)(2,1)S(1)} all-gather(bf16[64,1024]{1,0:T(8,128)(2,1)} %param.6), channel_id=1, replica_groups=mesh['row'=8,'col'=4] {'col'}, dimensions={0}, use_global_device_ids=true | all-gather | bytes 655360 | tf_op jit(solution)/shard_map/all_gather | solution.py:14
  16.8 62.4 %all-gather.2.cloned.1.call-done = bf16[256,7168]{1,0:T(8,128)(2,1)} async-done(((bf16[32,7168]{1,0:T(8,128)(2,1)}), bf16[256,7168]{1,0:T(8,128)(2,1)}) %all-gather.2.cloned.1.call-update) | async-done | bytes 3670032 | tf_op jit(solution)/shard_map/all_gather | solution.py:17
  79.1 13.7 %fusion.28 = f32[1024,7168]{1,0:T(8,128)} fusion(bf16[256,1024]{1,0:T(8,128)(2,1)S(1)} %all_gather.6, bf16[256,7168]{1,0:T(8,128)(2,1)} %all-gather.2.cloned.1.call-done), kind=kOutput, calls=%fused_computation.22 | convolution fusion | flops 3758096384 | bytes 33554432 | tf_op jit(solution)/shard_map/dot_general | solution.py:15
  92.8 0.0 copy-start.1
  92.8 35.5 %multiply_reduce_fusion = f32[3]{0:T(128)S(1)} fusion(f32[3,1024,7168]{2,1,0:T(8,128)} %param.8, f32[1024,7168]{1,0:T(8,128)} %fusion.28), kind=kLoop, calls=%fused_computation | loop fusion | flops 44040188 | bytes 117440528 | tf_op jit(solution)/shard_map/reduce_sum | solution.py:21
  128.4 5.7 %psum.21 = f32[3]{0:T(128)S(1)} all-reduce(f32[3]{0:T(128)S(1)} %multiply_reduce_fusion), channel_id=1, replica_groups=mesh['row'=8,'col'=4] {'col'}, use_global_device_ids=true, to_apply=%region_1.0 | all-reduce | flops 3 | bytes 24 | tf_op jit(solution)/shard_map/psum | solution.py:22
  134.0 4.0 %all-to-all-start = ((bf16[8,8,1024]{2,0,1:T(8,128)(2,1)}), bf16[8,8,1024]{2,0,1:T(8,128)(2,1)S(1)}, u32[]{:S(2)}, u32[]{:S(2)}) async-start(bf16[8,8,1024]{2,0,1:T(8,128)(2,1)} %bitcast.1), calls=%async_computation | async-start | bytes 262144 | tf_op jit(solution)/shard_map/all_to_all | solution.py:24
  138.1 0.0 reduce-scatter.2.cloned.1.call-start
  138.1 22.0 %psum.22 = f32[3]{0:T(128)S(1)} all-reduce(f32[3]{0:T(128)S(1)} %psum.21), channel_id=1, replica_groups=mesh['row'=8,'col'=4] {'row'}, use_global_device_ids=true, to_apply=%region_2.0 | all-reduce | flops 3 | bytes 24 | tf_op jit(solution)/shard_map/psum | solution.py:22
  160.1 0.0 copy-done.1
  160.1 0.7 fusion.27
  160.7 0.0 all-to-all-done
  160.8 15.6 %fusion.15 = f32[64,7168]{1,0:T(8,128)S(1)} fusion(f32[3,1024,7168]{2,1,0:T(8,128)} %param.8, f32[]{:T(128)} %bitcast.5, bf16[8,8,1024]{2,0,1:T(8,128)(2,1)S(1)} %all-to-all-done), kind=kOutput, calls=%fused_computation.12 | convolution fusion | flops 5637603328 | bytes 31326720 | tf_op jit(solution)/shard_map/dot_general | solution.py:30
  176.4 18.0 %fusion.12 = f32[64,7168]{1,0:T(8,128)S(1)} fusion(f32[64,7168]{1,0:T(8,128)S(1)} %fusion.15, f32[3,1024,7168]{2,1,0:T(8,128)} %param.8, f32[]{:T(128)} %bitcast, bf16[8,8,1024]{2,0,1:T(8,128)(2,1)S(1)} %all-to-all-done), kind=kOutput, calls=%fused_computation.11 | convolution fusion | flops 5638062080 | bytes 33161728 | tf_op jit(solution)/shard_map/dot_general | solution.py:30
  194.3 0.0 copy-start
  194.3 17.5 %fusion.21 = f32[64,7168]{1,0:T(8,128)} fusion(f32[64,7168]{1,0:T(8,128)S(1)} %fusion.12, f32[3,1024,7168]{2,1,0:T(8,128)} %param.8, f32[]{:T(128)} %bitcast.8, bf16[8,8,1024]{2,0,1:T(8,128)(2,1)S(1)} %all-to-all-done), kind=kOutput, calls=%fused_computation.14 | convolution fusion | flops 5638062080 | bytes 33161728 | tf_op jit(solution)/shard_map/dot_general | solution.py:30
  211.8 0.0 reduce-scatter.2.cloned.1.call-update
  211.9 64.1 %reduce-scatter.2.cloned.1.call-done = f32[8,7168]{1,0:T(8,128)} async-done(((f32[64,7168]{1,0:T(8,128)}), f32[8,7168]{1,0:T(8,128)}) %reduce-scatter.2.cloned.1.call-update) | async-done | bytes 229392 | tf_op jit(solution)/shard_map/reduce_scatter | solution.py:31
  275.9 0.0 copy-done
  275.9 1.8 multiply_reduce_fusion.1
  277.8 6.2 %psum.23 = f32[8]{0:T(128)} all-reduce(f32[8]{0:T(128)S(1)} %broadcast_multiply_fusion), channel_id=1, replica_groups=mesh['row'=8,'col'=4] {'col'}, use_global_device_ids=true, to_apply=%region_5.0 | all-reduce | flops 8 | bytes 64 | tf_op jit(solution)/shard_map/psum | solution.py:33
  (2 shorter events, 0.0 us)
Async XLA Ops:
  7.2 72.0 %all-gather.2.cloned.1.call-start = ((), (), s32[]{:S(2)}) async-start(), calls=%async_computation.2 | async-start | bytes 4128768 | tf_op jit(solution)/shard_map/all_gather | solution.py:17
  92.8 67.2 %copy-start.1 = (f32[3]{0:T(128)S(1)}, f32[3]{0:T(128)}, u32[]{:S(2)}) copy-start(f32[3]{0:T(128)} %param.9) | copy-start | bytes 40
  134.0 26.7 %all-to-all-start = ((bf16[8,8,1024]{2,0,1:T(8,128)(2,1)}), bf16[8,8,1024]{2,0,1:T(8,128)(2,1)S(1)}, u32[]{:S(2)}, u32[]{:S(2)}) async-start(bf16[8,8,1024]{2,0,1:T(8,128)(2,1)} %bitcast.1), calls=%async_computation | async-start | bytes 262144 | tf_op jit(solution)/shard_map/all_to_all | solution.py:24
  138.1 137.9 %reduce-scatter.2.cloned.1.call-start = ((), (), s32[]{:S(2)}) async-start(), calls=%async_computation.3 | async-start | bytes 2064384 | tf_op jit(solution)/shard_map/reduce_scatter | solution.py:31
  194.3 81.6 %copy-start = (bf16[8,7168]{1,0:T(8,128)(2,1)S(1)}, bf16[8,7168]{1,0:T(8,128)(2,1)}, u32[]{:S(2)}) copy-start(bf16[8,7168]{1,0:T(8,128)(2,1)} %param.11) | copy-start | bytes 344068
Sparse Core Ops, SparseCore 0:
  10.2 68.9 all-gather.1
  212.0 63.9 reduce-scatter.1
